TPU v7x, 32 devices: a whole 2x2x4 slice. The times are simulated.
32 devices in a mesh: layer: 4 (over y, x), col: 8 (over z, core).
Axes of the slice: x: 2, y: 2, z: 4, core: 2. Of those that a mesh axis runs over, the one named last changes fastest.
Arguments:
- inputs: bfloat16 [4, 128, 4096], replicated, may hold values from -6 to 6
- w_input: bfloat16 [4, 4096, 4, 4096], P('layer', None, None, 'col'), may hold values from -0.09375 to 0.09375
- w_recur: bfloat16 [4, 4096, 4, 4096], P('layer', None, None, 'col'), may hold values from -0.09375 to 0.09375
- bias: float32 [4, 4, 4096], P('layer', None, 'col'), may hold values from -1 to 2
- h_start: bfloat16 [4, 128, 4096], P('layer', None, 'col'), may hold values from -3 to 3
- c_start: float32 [4, 128, 4096], P('layer', None, 'col'), may hold values from -6 to 6
Outputs:
- hidden_seq: bfloat16 [4, 4, 128, 4096], P('layer', None, None, 'col')
- cell_final: float32 [4, 128, 4096], P('layer', None, 'col')
All inputs are finite; a program needn't handle non-finite values.
Results may differ from a plain program's by a relative error of at most 0.0024.
Values may be sent and summed in bfloat16 or wider, within the bound.
A program may use at most 128 MiB of HBM per device.

v0:
```python
import jax
import jax.numpy as jnp
from jax import lax
from jax.sharding import PartitionSpec as P


def passed_along(value, axis, steps):
    count = lax.axis_size(axis)
    first, last = (max(0, -steps), min(count, count - steps))
    return lax.ppermute(value, axis, [(source, source + steps) for source in range(first, last)])


def body(inputs, w_input, w_recur, bias, h_start, c_start):
    steps = inputs.shape[0]
    batch = inputs.shape[1]
    width = inputs.shape[2]
    local = w_input.shape[3]
    span = steps // 4
    count = steps // span
    groups = lax.axis_size("layer")
    rounds = count + groups - 1
    section = lax.axis_index("layer")
    weight_in = w_input[0].reshape(width, 4 * local)
    weight_rec = w_recur[0].reshape(width, 4 * local)
    offset = bias[0].reshape(4 * local)
    hidden_full = lax.all_gather(h_start[0], "col", axis=1, tiled=True)
    cell = c_start[0]
    sequence = jnp.zeros((steps, batch, local), jnp.bfloat16)
    arrived = jnp.zeros((span, batch, width), jnp.bfloat16)

    def advance(carry, z_in):
        hidden_prev, cell_prev = carry
        gates = z_in + jnp.dot(hidden_prev, weight_rec, preferred_element_type=jnp.float32)
        gates = gates.reshape(batch, 4, local)
        cell_new = jax.nn.sigmoid(gates[:, 1]) * cell_prev + jax.nn.sigmoid(gates[:, 0]) * jnp.tanh(
            gates[:, 2]
        )
        hidden_new = (jax.nn.sigmoid(gates[:, 3]) * jnp.tanh(cell_new)).astype(jnp.bfloat16)
        hidden_wide = lax.all_gather(hidden_new, "col", axis=1, tiled=True)
        return ((hidden_wide, cell_new), (hidden_new, hidden_wide))

    for turn in range(rounds):
        block_id = turn - section
        valid = jnp.logical_and(block_id >= 0, block_id < count)
        start = jnp.clip(block_id, 0, count - 1) * span
        own_block = lax.dynamic_slice_in_dim(inputs, start, span, 0)
        source = jnp.where(section == 0, own_block, arrived)
        projected = (
            jnp.dot(
                source.reshape(span * batch, width), weight_in, preferred_element_type=jnp.float32
            )
            + offset
        )
        projected = projected.reshape(span, batch, 4 * local)
        (hidden_next, cell_next), (shards, wides) = lax.scan(
            advance, (hidden_full, cell), projected
        )
        hidden_full = jnp.where(valid, hidden_next, hidden_full)
        cell = jnp.where(valid, cell_next, cell)
        sequence = jnp.where(
            valid, lax.dynamic_update_slice_in_dim(sequence, shards, start, 0), sequence
        )
        if turn + 1 < rounds:
            received = passed_along(shards, "layer", 1)
            arrived = lax.all_gather(received, "col", axis=2, tiled=True)
    return (sequence[None], cell[None])


def solution(mesh):
    in_specs = (
        P(),
        P("layer", None, None, "col"),
        P("layer", None, None, "col"),
        P("layer", None, "col"),
        P("layer", None, "col"),
        P("layer", None, "col"),
    )
    out_specs = (P("layer", None, None, "col"), P("layer", None, "col"))
    return jax.shard_map(body, mesh=mesh, in_specs=in_specs, out_specs=out_specs, check_vma=False)
```

profile of v0, /device:TPU:6, one launch (start us, length us, event | category | flops | bytes accessed | tf_op | source)
XLA Modules:
  0.0 450.3 jit_solution(1819920880127915274)
XLA Ops:
  8.7 18.1 %copy.64 = bf16[512,8,4,512]{3,1,2,0:T(8,128)(2,1)} copy(bf16[512,8,4,512]{3,2,1,0:T(4,128)(2,1)} %bitcast.365) | data formatting | bytes 33554432
  26.8 9.5 %copy.66 = bf16[512,8,4,512]{3,1,2,0:T(8,128)(2,1)} copy(bf16[512,8,4,512]{3,2,1,0:T(4,128)(2,1)S(1)} %bitcast.366) | data formatting | bytes 33554432
  36.3 8.4 %convolution_add_fusion.7 = f32[128,2048]{1,0:T(8,128)S(1)} fusion(bf16[4096,2048]{1,0:T(8,128)(2,1)} %bitcast.351, bf16[4,128,4096]{2,1,0:T(8,128)(2,1)} %param.6, s32[]{:T(128)S(6)} %min.22, pred[]{:T(512)S(6)} %eq.2, f32[2048]{0:T(1024)S(1)} %bitcast.368), kind=kOutput, calls=%fused_computation.13 | convolution fusion | flops 2148270080 | bytes 18882564 | tf_op jit(solution)/shard_map/dot_general | solution.py:49
  44.8 8.5 %convolution_add_fusion.6 = f32[128,2048]{1,0:T(8,128)S(1)} fusion(f32[128,2048]{1,0:T(8,128)S(1)} %convolution_add_fusion.7, bf16[4096,2048]{1,0:T(8,128)(2,1)} %bitcast.358, bf16[1,128,4096]{2,1,0:T(8,128)(2,1)} %all-gather.39.cloned.1.call-done), kind=kOutput, calls=%fused_computation.12 | convolution fusion | flops 2147745792 | bytes 19922944 | tf_op jit(solution)/shard_map/while/body/eval_jaxpr/dot_general | solution.py:33
  56.0 1.3 collective-permute-start
  57.3 5.9 %collective-permute-done = bf16[1,128,512]{2,1,0:T(8,128)(2,1)S(1)} collective-permute-done((bf16[1,128,512]{2,1,0:T(8,128)(2,1)S(1)}, bf16[1,128,512]{2,1,0:T(8,128)(2,1)S(1)}, u32[]{:S(2)}, u32[]{:S(2)}) %collective-permute-start) | collective-permute-done | bytes 131104 | tf_op jit(solution)/shard_map/ppermute | solution.py:10
  64.5 14.9 %all-gather.17.cloned.1.call-done = bf16[128,4096]{1,0:T(8,128)(2,1)} async-done(((bf16[128,512]{1,0:T(8,128)(2,1)}), bf16[128,4096]{1,0:T(8,128)(2,1)}) %all-gather.17.cloned.1.call-update) | async-done | bytes 1048592 | tf_op jit(solution)/shard_map/while/body/eval_jaxpr/all_gather | solution.py:39
  79.3 1.3 bitcast_select_fusion
  80.7 9.1 %fusion.159 = f32[128,2048]{1,0:T(8,128)} fusion(bf16[128,4096]{1,0:T(8,128)(2,1)S(1)} %bitcast_select_fusion, bf16[4096,2048]{1,0:T(8,128)(2,1)} %bitcast.359), kind=kOutput, calls=%fused_computation.241 | convolution fusion | flops 2147483648 | bytes 18874368 | tf_op jit(solution)/shard_map/while/body/eval_jaxpr/dot_general | solution.py:33
  89.8 13.6 %all-gather.15.cloned.1.call-done = bf16[1,128,4096]{2,1,0:T(8,128)(2,1)} async-done(((bf16[1,128,512]{2,1,0:T(8,128)(2,1)}), bf16[1,128,4096]{2,1,0:T(8,128)(2,1)}) %all-gather.15.cloned.1.call-update) | async-done | bytes 1048592 | tf_op jit(solution)/shard_map/all_gather | solution.py:65
  103.4 10.0 %fusion.5 = f32[128,2048]{1,0:T(8,128)} fusion(f32[128,2048]{1,0:T(8,128)} %fusion.159, bf16[4096,2048]{1,0:T(8,128)(2,1)} %bitcast.352, bf16[1,128,4096]{2,1,0:T(8,128)(2,1)} %all-gather.15.cloned.1.call-done, bf16[4,128,4096]{2,1,0:T(8,128)(2,1)} %param.6, s32[]{:T(128)S(6)} %min.23, pred[]{:T(512)S(6)} %eq.2, f32[2048]{0:T(1024)S(1)} %bitcast.369), kind=kOutput, calls=%fused_computation.11 | convolution fusion | flops 2148532224 | bytes 20979716 | tf_op jit(solution)/shard_map/dot_general | solution.py:49
  113.4 2.9 reshape.901
  116.3 3.5 fusion.157
  119.7 1.1 fusion.127
  121.2 1.3 collective-permute-start.1
  122.5 6.2 %collective-permute-done.1 = bf16[1,128,512]{2,1,0:T(8,128)(2,1)S(1)} collective-permute-done((bf16[1,128,512]{2,1,0:T(8,128)(2,1)S(1)}, bf16[1,128,512]{2,1,0:T(8,128)(2,1)S(1)}, u32[]{:S(2)}, u32[]{:S(2)}) %collective-permute-start.1) | collective-permute-done | bytes 131104 | tf_op jit(solution)/shard_map/ppermute | solution.py:10
  129.6 13.4 %all-gather.21.cloned.1.call-done = bf16[128,4096]{1,0:T(8,128)(2,1)} async-done(((bf16[128,512]{1,0:T(8,128)(2,1)}), bf16[128,4096]{1,0:T(8,128)(2,1)}) %all-gather.21.cloned.1.call-update) | async-done | bytes 1048592 | tf_op jit(solution)/shard_map/while/body/eval_jaxpr/all_gather | solution.py:39
  143.0 9.1 %fusion.39 = f32[128,2048]{1,0:T(8,128)} fusion(bf16[4096,2048]{1,0:T(8,128)(2,1)} %bitcast.360, bf16[128,4096]{1,0:T(8,128)(2,1)} %all-gather.21.cloned.1.call-done, bf16[128,4096]{1,0:T(8,128)(2,1)S(1)} %bitcast_select_fusion, pred[]{:T(512)S(6)} %and.23), kind=kOutput, calls=%fused_computation.52 | convolution fusion | flops 2148007936 | bytes 19922944 | tf_op jit(solution)/shard_map/while/body/eval_jaxpr/dot_general | solution.py:33
  152.2 14.2 %all-gather.19.cloned.1.call-done = bf16[1,128,4096]{2,1,0:T(8,128)(2,1)} async-done(((bf16[1,128,512]{2,1,0:T(8,128)(2,1)}), bf16[1,128,4096]{2,1,0:T(8,128)(2,1)}) %all-gather.19.cloned.1.call-update) | async-done | bytes 1048592 | tf_op jit(solution)/shard_map/all_gather | solution.py:65
  166.4 10.0 %fusion.4 = f32[128,2048]{1,0:T(8,128)} fusion(f32[128,2048]{1,0:T(8,128)} %fusion.39, bf16[4096,2048]{1,0:T(8,128)(2,1)} %bitcast.353, bf16[1,128,4096]{2,1,0:T(8,128)(2,1)} %all-gather.19.cloned.1.call-done, bf16[4,128,4096]{2,1,0:T(8,128)(2,1)} %param.6, s32[]{:T(128)S(6)} %min.24, pred[]{:T(512)S(6)} %eq.2, f32[2048]{0:T(1024)S(1)} %bitcast.370), kind=kOutput, calls=%fused_computation.9 | convolution fusion | flops 2148532224 | bytes 20979716 | tf_op jit(solution)/shard_map/dot_general | solution.py:49
  176.4 2.9 reshape.903
  179.3 3.9 fusion.156
  183.9 2.0 fusion.125
  186.0 2.0 select_dynamic-update-slice_fusion.3
  188.0 1.3 collective-permute-start.2
  189.3 6.2 %collective-permute-done.2 = bf16[1,128,512]{2,1,0:T(8,128)(2,1)S(1)} collective-permute-done((bf16[1,128,512]{2,1,0:T(8,128)(2,1)S(1)}, bf16[1,128,512]{2,1,0:T(8,128)(2,1)S(1)}, u32[]{:S(2)}, u32[]{:S(2)}) %collective-permute-start.2) | collective-permute-done | bytes 131104 | tf_op jit(solution)/shard_map/ppermute | solution.py:10
  196.5 11.5 %all-gather.25.cloned.1.call-done = bf16[128,4096]{1,0:T(8,128)(2,1)} async-done(((bf16[128,512]{1,0:T(8,128)(2,1)}), bf16[128,4096]{1,0:T(8,128)(2,1)}) %all-gather.25.cloned.1.call-update) | async-done | bytes 1048592 | tf_op jit(solution)/shard_map/while/body/eval_jaxpr/all_gather | solution.py:39
  208.1 9.1 %fusion.160 = f32[128,2048]{1,0:T(8,128)} fusion(bf16[128,4096]{1,0:T(8,128)(2,1)S(1)} %broadcast_select_fusion.2, bf16[4096,2048]{1,0:T(8,128)(2,1)} %bitcast.361), kind=kOutput, calls=%fused_computation.242 | convolution fusion | flops 2147483648 | bytes 18874368 | tf_op jit(solution)/shard_map/while/body/eval_jaxpr/dot_general | solution.py:33
  217.2 14.2 %all-gather.23.cloned.1.call-done = bf16[1,128,4096]{2,1,0:T(8,128)(2,1)} async-done(((bf16[1,128,512]{2,1,0:T(8,128)(2,1)}), bf16[1,128,4096]{2,1,0:T(8,128)(2,1)}) %all-gather.23.cloned.1.call-update) | async-done | bytes 1048592 | tf_op jit(solution)/shard_map/all_gather | solution.py:65
  231.4 10.0 %fusion.3 = f32[128,2048]{1,0:T(8,128)} fusion(f32[128,2048]{1,0:T(8,128)} %fusion.160, bf16[4096,2048]{1,0:T(8,128)(2,1)} %bitcast.354, bf16[1,128,4096]{2,1,0:T(8,128)(2,1)} %all-gather.23.cloned.1.call-done, bf16[4,128,4096]{2,1,0:T(8,128)(2,1)} %param.6, s32[]{:T(128)S(6)} %min.25, pred[]{:T(512)S(6)} %eq.2, f32[2048]{0:T(1024)S(1)} %bitcast.371), kind=kOutput, calls=%fused_computation.7 | convolution fusion | flops 2148532224 | bytes 20979716 | tf_op jit(solution)/shard_map/dot_general | solution.py:49
  241.4 2.9 reshape.905
  244.3 3.9 fusion.155
  248.3 2.2 fusion.123
  250.6 1.2 select_dynamic-update-slice_fusion.2
  251.8 1.3 collective-permute-start.3
  253.1 6.2 %collective-permute-done.3 = bf16[1,128,512]{2,1,0:T(8,128)(2,1)S(1)} collective-permute-done((bf16[1,128,512]{2,1,0:T(8,128)(2,1)S(1)}, bf16[1,128,512]{2,1,0:T(8,128)(2,1)S(1)}, u32[]{:S(2)}, u32[]{:S(2)}) %collective-permute-start.3) | collective-permute-done | bytes 131104 | tf_op jit(solution)/shard_map/ppermute | solution.py:10
  260.3 12.2 %all-gather.29.cloned.1.call-done = bf16[128,4096]{1,0:T(8,128)(2,1)} async-done(((bf16[128,512]{1,0:T(8,128)(2,1)}), bf16[128,4096]{1,0:T(8,128)(2,1)}) %all-gather.29.cloned.1.call-update) | async-done | bytes 1048592 | tf_op jit(solution)/shard_map/while/body/eval_jaxpr/all_gather | solution.py:39
  272.5 9.5 %fusion.40 = f32[128,2048]{1,0:T(8,128)} fusion(bf16[4096,2048]{1,0:T(8,128)(2,1)} %bitcast.362, bf16[128,4096]{1,0:T(8,128)(2,1)} %all-gather.29.cloned.1.call-done, bf16[128,4096]{1,0:T(8,128)(2,1)S(1)} %broadcast_select_fusion.2, pred[]{:T(512)S(6)} %and.25), kind=kOutput, calls=%fused_computation.53 | convolution fusion | flops 2148007936 | bytes 19922944 | tf_op jit(solution)/shard_map/while/body/eval_jaxpr/dot_general | solution.py:33
  282.0 14.6 %all-gather.27.cloned.1.call-done = bf16[1,128,4096]{2,1,0:T(8,128)(2,1)} async-done(((bf16[1,128,512]{2,1,0:T(8,128)(2,1)}), bf16[1,128,4096]{2,1,0:T(8,128)(2,1)}) %all-gather.27.cloned.1.call-update) | async-done | bytes 1048592 | tf_op jit(solution)/shard_map/all_gather | solution.py:65
  296.6 10.0 %fusion.2 = f32[128,2048]{1,0:T(8,128)} fusion(f32[128,2048]{1,0:T(8,128)} %fusion.40, bf16[4096,2048]{1,0:T(8,128)(2,1)} %bitcast.355, bf16[1,128,4096]{2,1,0:T(8,128)(2,1)} %all-gather.27.cloned.1.call-done, bf16[4,128,4096]{2,1,0:T(8,128)(2,1)} %param.6, s32[]{:T(128)S(6)} %min.26, pred[]{:T(512)S(6)} %eq.2, f32[2048]{0:T(1024)S(1)} %bitcast.372), kind=kOutput, calls=%fused_computation.5 | convolution fusion | flops 2148532224 | bytes 20979716 | tf_op jit(solution)/shard_map/dot_general | solution.py:49
  306.6 2.9 reshape.907
  309.5 3.9 fusion.154
  314.1 1.9 fusion.121
  316.2 2.0 select_dynamic-update-slice_fusion.1
  318.2 1.3 collective-permute-start.4
  319.5 6.2 %collective-permute-done.4 = bf16[1,128,512]{2,1,0:T(8,128)(2,1)S(1)} collective-permute-done((bf16[1,128,512]{2,1,0:T(8,128)(2,1)S(1)}, bf16[1,128,512]{2,1,0:T(8,128)(2,1)S(1)}, u32[]{:S(2)}, u32[]{:S(2)}) %collective-permute-start.4) | collective-permute-done | bytes 131104 | tf_op jit(solution)/shard_map/ppermute | solution.py:10
  326.9 11.2 %all-gather.33.cloned.1.call-done = bf16[128,4096]{1,0:T(8,128)(2,1)} async-done(((bf16[128,512]{1,0:T(8,128)(2,1)}), bf16[128,4096]{1,0:T(8,128)(2,1)}) %all-gather.33.cloned.1.call-update) | async-done | bytes 1048592 | tf_op jit(solution)/shard_map/while/body/eval_jaxpr/all_gather | solution.py:39
  338.1 1.7 broadcast_select_fusion
  339.8 9.1 %fusion.161 = f32[128,2048]{1,0:T(8,128)} fusion(bf16[128,4096]{1,0:T(8,128)(2,1)S(1)} %broadcast_select_fusion, bf16[4096,2048]{1,0:T(8,128)(2,1)} %bitcast.363), kind=kOutput, calls=%fused_computation.243 | convolution fusion | flops 2147483648 | bytes 18874368 | tf_op jit(solution)/shard_map/while/body/eval_jaxpr/dot_general | solution.py:33
  348.9 12.7 %all-gather.31.cloned.1.call-done = bf16[1,128,4096]{2,1,0:T(8,128)(2,1)} async-done(((bf16[1,128,512]{2,1,0:T(8,128)(2,1)}), bf16[1,128,4096]{2,1,0:T(8,128)(2,1)}) %all-gather.31.cloned.1.call-update) | async-done | bytes 1048592 | tf_op jit(solution)/shard_map/all_gather | solution.py:65
  361.6 10.0 %fusion.1 = f32[128,2048]{1,0:T(8,128)} fusion(f32[128,2048]{1,0:T(8,128)} %fusion.161, bf16[4096,2048]{1,0:T(8,128)(2,1)} %bitcast.356, bf16[1,128,4096]{2,1,0:T(8,128)(2,1)} %all-gather.31.cloned.1.call-done, bf16[4,128,4096]{2,1,0:T(8,128)(2,1)} %param.6, s32[]{:T(128)S(6)} %min.27, pred[]{:T(512)S(6)} %eq.2, f32[2048]{0:T(1024)S(1)} %bitcast.373), kind=kOutput, calls=%fused_computation.3 | convolution fusion | flops 2148532224 | bytes 20979716 | tf_op jit(solution)/shard_map/dot_general | solution.py:49
  371.6 2.9 reshape.909
  374.5 3.9 fusion.153
  379.1 2.0 fusion.119
  381.3 1.4 select_dynamic-update-slice_fusion
  382.7 1.5 collective-permute-start.5
  384.1 6.0 %collective-permute-done.5 = bf16[1,128,512]{2,1,0:T(8,128)(2,1)S(1)} collective-permute-done((bf16[1,128,512]{2,1,0:T(8,128)(2,1)S(1)}, bf16[1,128,512]{2,1,0:T(8,128)(2,1)S(1)}, u32[]{:S(2)}, u32[]{:S(2)}) %collective-permute-start.5) | collective-permute-done | bytes 131104 | tf_op jit(solution)/shard_map/ppermute | solution.py:10
  391.7 11.5 %all-gather.37.cloned.1.call-done = bf16[128,4096]{1,0:T(8,128)(2,1)} async-done(((bf16[128,512]{1,0:T(8,128)(2,1)}), bf16[128,4096]{1,0:T(8,128)(2,1)}) %all-gather.37.cloned.1.call-update) | async-done | bytes 1048592 | tf_op jit(solution)/shard_map/while/body/eval_jaxpr/all_gather | solution.py:39
  403.2 9.5 %fusion.14 = f32[128,2048]{1,0:T(8,128)} fusion(bf16[4096,2048]{1,0:T(8,128)(2,1)} %bitcast.364, bf16[128,4096]{1,0:T(8,128)(2,1)} %all-gather.37.cloned.1.call-done, bf16[128,4096]{1,0:T(8,128)(2,1)S(1)} %broadcast_select_fusion, pred[]{:T(512)S(6)} %and.27), kind=kOutput, calls=%fused_computation.23 | convolution fusion | flops 2148007936 | bytes 19922944 | tf_op jit(solution)/shard_map/while/body/eval_jaxpr/dot_general | solution.py:33
  412.7 14.6 %all-gather.35.cloned.1.call-done = bf16[1,128,4096]{2,1,0:T(8,128)(2,1)} async-done(((bf16[1,128,512]{2,1,0:T(8,128)(2,1)}), bf16[1,128,4096]{2,1,0:T(8,128)(2,1)}) %all-gather.35.cloned.1.call-update) | async-done | bytes 1048592 | tf_op jit(solution)/shard_map/all_gather | solution.py:65
  427.3 9.1 %fusion = f32[128,2048]{1,0:T(8,128)S(1)} fusion(f32[128,2048]{1,0:T(8,128)} %fusion.14, bf16[4096,2048]{1,0:T(8,128)(2,1)} %bitcast.357, bf16[1,128,4096]{2,1,0:T(8,128)(2,1)} %all-gather.35.cloned.1.call-done, bf16[4,128,4096]{2,1,0:T(8,128)(2,1)} %param.6, s32[]{:T(128)S(6)} %min.28, pred[]{:T(512)S(6)} %eq.2, f32[2048]{0:T(1024)S(1)} %bitcast.374), kind=kOutput, calls=%fused_computation.1 | convolution fusion | flops 2148532224 | bytes 20979716 | tf_op jit(solution)/shard_map/dot_general | solution.py:49
  436.3 1.7 reshape.911
  438.0 3.6 fusion.152
  441.7 1.1 broadcast_select_fusion.6
  (91 shorter events, 14.4 us)
Async XLA Ops:
  7.2 37.6 %all-gather.39.cloned.1.call-start = ((), (), s32[]{:S(2)}) async-start(), calls=%async_computation.12 | async-start | bytes 1179648 | tf_op jit(solution)/shard_map/all_gather | solution.py:26
  7.9 71.4 %all-gather.17.cloned.1.call-start = ((), (), s32[]{:S(2)}) async-start(), calls=%async_computation.1 | async-start | bytes 1179648 | tf_op jit(solution)/shard_map/while/body/eval_jaxpr/all_gather | solution.py:39
  8.7 18.1 %copy-start = (bf16[1,4096,4,512]{3,2,1,0:T(4,128)(2,1)S(1)}, bf16[1,4096,4,512]{3,2,1,0:T(4,128)(2,1)}, u32[]{:S(2)}) copy-start(bf16[1,4096,4,512]{3,2,1,0:T(4,128)(2,1)} %param.8) | copy-start | bytes 50331652
  44.7 10.0 %copy-start.3 = (f32[1,128,512]{2,1,0:T(8,128)S(1)}, f32[1,128,512]{2,1,0:T(8,128)}, u32[]{:S(2)}) copy-start(f32[1,128,512]{2,1,0:T(8,128)} %param.11) | copy-start | bytes 786436
  55.7 47.6 %all-gather.15.cloned.1.call-start = ((), (), s32[]{:S(2)}) async-start(), calls=%async_computation | async-start | bytes 1179648 | tf_op jit(solution)/shard_map/all_gather | solution.py:65
  56.0 7.2 %collective-permute-start = (bf16[1,128,512]{2,1,0:T(8,128)(2,1)S(1)}, bf16[1,128,512]{2,1,0:T(8,128)(2,1)S(1)}, u32[]{:S(2)}, u32[]{:S(2)}) collective-permute-start(bf16[1,128,512]{2,1,0:T(8,128)(2,1)S(1)} %get-tuple-element.137), channel_id=1, source_target_pairs={{0,8},{8,16},{16,24},{1,9},{9,17},{17,25},{2,10},{10,18},{18,26},{... | collective-permute-start | bytes 393224 | tf_op jit(solution)/shard_map/ppermute | solution.py:10
  63.2 0.7 copy-start.23
  63.9 79.1 %all-gather.21.cloned.1.call-start = ((), (), s32[]{:S(2)}) async-start(), calls=%async_computation.3 | async-start | bytes 1179648 | tf_op jit(solution)/shard_map/while/body/eval_jaxpr/all_gather | solution.py:39
  120.8 65.2 %copy-start.4 = (f32[128,1,512]{2,0,1:T(8,128)}, f32[128,1,512]{2,0,1:T(8,128)S(1)}, u32[]{:S(2)}) copy-start(f32[128,1,512]{2,0,1:T(8,128)S(1)} %get-tuple-element.125) | copy-start | bytes 786436
  120.9 45.5 %all-gather.19.cloned.1.call-start = ((), (), s32[]{:S(2)}) async-start(), calls=%async_computation.2 | async-start | bytes 1179648 | tf_op jit(solution)/shard_map/all_gather | solution.py:65
  121.2 7.5 %collective-permute-start.1 = (bf16[1,128,512]{2,1,0:T(8,128)(2,1)S(1)}, bf16[1,128,512]{2,1,0:T(8,128)(2,1)S(1)}, u32[]{:S(2)}, u32[]{:S(2)}) collective-permute-start(bf16[1,128,512]{2,1,0:T(8,128)(2,1)S(1)} %get-tuple-element.133), channel_id=1, source_target_pairs={{0,8},{8,16},{16,24},{1,9},{9,17},{17,25},{2,10},{10,18},{18,26},{... | collective-permute-start | bytes 393224 | tf_op jit(solution)/shard_map/ppermute | solution.py:10
  128.7 0.6 copy-start.25
  129.4 78.6 %all-gather.25.cloned.1.call-start = ((), (), s32[]{:S(2)}) async-start(), calls=%async_computation.5 | async-start | bytes 1179648 | tf_op jit(solution)/shard_map/while/body/eval_jaxpr/all_gather | solution.py:39
  183.2 0.7 copy-start.18
  185.9 45.5 %all-gather.23.cloned.1.call-start = ((), (), s32[]{:S(2)}) async-start(), calls=%async_computation.4 | async-start | bytes 1179648 | tf_op jit(solution)/shard_map/all_gather | solution.py:65
  188.0 8.4 %copy-start.6 = (bf16[4,128,512]{2,1,0:T(8,128)(2,1)}, bf16[4,128,512]{2,1,0:T(8,128)(2,1)S(1)}, u32[]{:S(2)}) copy-start(bf16[4,128,512]{2,1,0:T(8,128)(2,1)S(1)} %get-tuple-element.120) | copy-start | bytes 1572868
  188.0 7.5 %collective-permute-start.2 = (bf16[1,128,512]{2,1,0:T(8,128)(2,1)S(1)}, bf16[1,128,512]{2,1,0:T(8,128)(2,1)S(1)}, u32[]{:S(2)}, u32[]{:S(2)}) collective-permute-start(bf16[1,128,512]{2,1,0:T(8,128)(2,1)S(1)} %get-tuple-element.121), channel_id=1, source_target_pairs={{0,8},{8,16},{16,24},{1,9},{9,17},{17,25},{2,10},{10,18},{18,26},{... | collective-permute-start | bytes 393224 | tf_op jit(solution)/shard_map/ppermute | solution.py:10
  195.5 0.6 copy-start.24
  196.2 76.3 %all-gather.29.cloned.1.call-start = ((), (), s32[]{:S(2)}) async-start(), calls=%async_computation.7 | async-start | bytes 1179648 | tf_op jit(solution)/shard_map/while/body/eval_jaxpr/all_gather | solution.py:39
  217.2 31.1 %copy-start.5 = (f32[128,1,512]{2,0,1:T(8,128)S(1)}, f32[128,1,512]{2,0,1:T(8,128)}, u32[]{:S(2)}) copy-start(f32[128,1,512]{2,0,1:T(8,128)} %copy-done.4) | copy-start | bytes 786436
  217.2 33.4 %copy-start.7 = (bf16[4,128,512]{2,1,0:T(8,128)(2,1)S(1)}, bf16[4,128,512]{2,1,0:T(8,128)(2,1)}, u32[]{:S(2)}) copy-start(bf16[4,128,512]{2,1,0:T(8,128)(2,1)} %copy-done.6) | copy-start | bytes 1572868
  217.2 33.4 %copy-start.14 = (f32[1,128,512]{2,1,0:T(8,128)S(1)}, f32[1,128,512]{2,1,0:T(8,128)}, u32[]{:S(2)}) copy-start(f32[1,128,512]{2,1,0:T(8,128)} %get-tuple-element.122) | copy-start | bytes 786436
  248.3 2.2 copy-start.20
  250.5 65.7 %copy-start.1 = (f32[128,1,512]{2,0,1:T(8,128)}, f32[128,1,512]{2,0,1:T(8,128)S(1)}, u32[]{:S(2)}) copy-start(f32[128,1,512]{2,0,1:T(8,128)S(1)} %get-tuple-element.109) | copy-start | bytes 786436
  250.5 46.1 %all-gather.27.cloned.1.call-start = ((), (), s32[]{:S(2)}) async-start(), calls=%async_computation.6 | async-start | bytes 1179648 | tf_op jit(solution)/shard_map/all_gather | solution.py:65
  251.8 7.5 %collective-permute-start.3 = (bf16[1,128,512]{2,1,0:T(8,128)(2,1)S(1)}, bf16[1,128,512]{2,1,0:T(8,128)(2,1)S(1)}, u32[]{:S(2)}, u32[]{:S(2)}) collective-permute-start(bf16[1,128,512]{2,1,0:T(8,128)(2,1)S(1)} %get-tuple-element.111), channel_id=1, source_target_pairs={{0,8},{8,16},{16,24},{1,9},{9,17},{17,25},{2,10},{10,18},{18,26},{... | collective-permute-start | bytes 393224 | tf_op jit(solution)/shard_map/ppermute | solution.py:10
  259.3 0.7 copy-start.26
  260.0 78.1 %all-gather.33.cloned.1.call-start = ((), (), s32[]{:S(2)}) async-start(), calls=%async_computation.9 | async-start | bytes 1179648 | tf_op jit(solution)/shard_map/while/body/eval_jaxpr/all_gather | solution.py:39
  282.0 34.2 %copy-start.15 = (f32[1,128,512]{2,1,0:T(8,128)S(1)}, f32[1,128,512]{2,1,0:T(8,128)}, u32[]{:S(2)}) copy-start(f32[1,128,512]{2,1,0:T(8,128)} %get-tuple-element.122) | copy-start | bytes 786436
  313.4 0.7 copy-start.17
  316.1 45.5 %all-gather.31.cloned.1.call-start = ((), (), s32[]{:S(2)}) async-start(), calls=%async_computation.8 | async-start | bytes 1179648 | tf_op jit(solution)/shard_map/all_gather | solution.py:65
  318.2 8.7 %copy-start.8 = (bf16[4,128,512]{2,1,0:T(8,128)(2,1)}, bf16[4,128,512]{2,1,0:T(8,128)(2,1)S(1)}, u32[]{:S(2)}) copy-start(bf16[4,128,512]{2,1,0:T(8,128)(2,1)S(1)} %get-tuple-element.98) | copy-start | bytes 1572868
  318.2 7.5 %collective-permute-start.4 = (bf16[1,128,512]{2,1,0:T(8,128)(2,1)S(1)}, bf16[1,128,512]{2,1,0:T(8,128)(2,1)S(1)}, u32[]{:S(2)}, u32[]{:S(2)}) collective-permute-start(bf16[1,128,512]{2,1,0:T(8,128)(2,1)S(1)} %get-tuple-element.99), channel_id=1, source_target_pairs={{0,8},{8,16},{16,24},{1,9},{9,17},{17,25},{2,10},{10,18},{18,26},{... | collective-permute-start | bytes 393224 | tf_op jit(solution)/shard_map/ppermute | solution.py:10
  325.7 0.7 copy-start.22
  326.4 76.8 %all-gather.37.cloned.1.call-start = ((), (), s32[]{:S(2)}) async-start(), calls=%async_computation.11 | async-start | bytes 1179648 | tf_op jit(solution)/shard_map/while/body/eval_jaxpr/all_gather | solution.py:39
  348.9 30.3 %copy-start.2 = (f32[128,1,512]{2,0,1:T(8,128)S(1)}, f32[128,1,512]{2,0,1:T(8,128)}, u32[]{:S(2)}) copy-start(f32[128,1,512]{2,0,1:T(8,128)} %copy-done.1) | copy-start | bytes 786436
  348.9 32.4 %copy-start.9 = (bf16[4,128,512]{2,1,0:T(8,128)(2,1)S(1)}, bf16[4,128,512]{2,1,0:T(8,128)(2,1)}, u32[]{:S(2)}) copy-start(bf16[4,128,512]{2,1,0:T(8,128)(2,1)} %copy-done.8) | copy-start | bytes 1572868
  378.4 0.7 copy-start.19
  378.5 34.2 %copy-start.10 = (f32[128,1,512]{2,1,0:T(1,128)}, f32[128,1,512]{2,1,0:T(1,128)S(1)}, u32[]{:S(2)}) copy-start(f32[128,1,512]{2,1,0:T(1,128)S(1)} %get-tuple-element.156) | copy-start | bytes 786436
  378.5 34.2 %copy-start.12 = (f32[128,1,512]{2,1,0:T(1,128)}, f32[128,1,512]{2,1,0:T(1,128)S(1)}, u32[]{:S(2)}) copy-start(f32[128,1,512]{2,1,0:T(1,128)S(1)} %get-tuple-element.157) | copy-start | bytes 786436
  381.2 46.1 %all-gather.35.cloned.1.call-start = ((), (), s32[]{:S(2)}) async-start(), calls=%async_computation.10 | async-start | bytes 1179648 | tf_op jit(solution)/shard_map/all_gather | solution.py:65
  382.7 7.5 %collective-permute-start.5 = (bf16[1,128,512]{2,1,0:T(8,128)(2,1)S(1)}, bf16[1,128,512]{2,1,0:T(8,128)(2,1)S(1)}, u32[]{:S(2)}, u32[]{:S(2)}) collective-permute-start(bf16[1,128,512]{2,1,0:T(8,128)(2,1)S(1)} %get-tuple-element.89), channel_id=1, source_target_pairs={{0,8},{8,16},{16,24},{1,9},{9,17},{17,25},{2,10},{10,18},{18,26},{... | collective-permute-start | bytes 393224 | tf_op jit(solution)/shard_map/ppermute | solution.py:10
  390.2 0.7 copy-start.21
  412.7 29.0 %copy-start.16 = (f32[1,128,512]{2,1,0:T(8,128)S(1)}, f32[1,128,512]{2,1,0:T(8,128)}, u32[]{:S(2)}) copy-start(f32[1,128,512]{2,1,0:T(8,128)} %get-tuple-element.100) | copy-start | bytes 786436
  427.3 14.4 %copy-start.11 = (f32[128,1,512]{2,1,0:T(1,128)S(1)}, f32[128,1,512]{2,1,0:T(1,128)}, u32[]{:S(2)}) copy-start(f32[128,1,512]{2,1,0:T(1,128)} %copy-done.10) | copy-start | bytes 786436
  427.3 14.4 %copy-start.13 = (f32[128,1,512]{2,1,0:T(1,128)S(1)}, f32[128,1,512]{2,1,0:T(1,128)}, u32[]{:S(2)}) copy-start(f32[128,1,512]{2,1,0:T(1,128)} %copy-done.12) | copy-start | bytes 786436
Sparse Core Ops, SparseCore 0:
  9.6 23.4 all-gather.38
  55.9 23.4 all-gather.16
  81.5 21.8 all-gather.14
  121.0 22.0 all-gather.20
  144.5 21.8 all-gather.18
  186.1 21.8 all-gather.24
  209.5 21.8 all-gather.22
  250.6 21.8 all-gather.28
  274.7 21.8 all-gather.26
  316.2 21.8 all-gather.32
  339.7 21.8 all-gather.30
  381.3 21.8 all-gather.36
  405.4 21.8 all-gather.34
where the time goes:
time: 459 us; the launch traced here: 450 us
  waiting for transfers between devices  196 us (43%)
  matrix products  131 us (29%)
  local copies, waits for them, and re-layouts  75.8 us (17%)
  other arithmetic  22.3 us (5%)
  between operations  14.5 us (3%)
  starting transfers between devices  10.1 us (2%)
    all_gather x6, waiting for transfers between devices, body(): arrived = lax.all_gather(received, 'col', axis=2, tiled=True)  84 us
    all_gather x6, waiting for transfers between devices, advance(): hidden_wide = lax.all_gather(hidden_new, 'col', axis=1, tiled=True)  74.7 us
    dot_general x7, matrix products, body(): jnp.dot(source.reshape(span * batch, width), weight_in, preferred_element...  67.5 us
    dot_general x7, matrix products, advance(): jnp.dot(hidden_prev, weight_rec, preferred_element_type=jnp.float32)  63.8 us
    ppermute x6, waiting for transfers between devices, passed_along(): lax.ppermute(value, axis, [(source, source + steps) for source in range(f...  36.8 us
    unnamed x58, local copies, waits for them, and re-layouts  35.2 us
    reshape x7, local copies, waits for them, and re-layouts, advance(): gates = gates.reshape(batch, 4, local)  17 us
    slice x5, local copies, waits for them, and re-layouts, advance(): gates[:, 0]  16 us
  transfers between devices with their start and end apart: 19, of which 18 were waited for; matrix products, arithmetic and copies ran while one was open for 23% of the time, Pallas kernels for 0%

commit v1 on v0

v1 whole, which is shorter than its diff:
```python
import functools

import jax
import jax.numpy as jnp
from jax import lax
from jax.experimental import pallas as pl
from jax.experimental.pallas import tpu as pltpu
from jax.sharding import PartitionSpec as P

MESH = pl.DeviceIdType.MESH
LEFT, RIGHT, SIBLING, NEXT = range(4)


def kernel(
    groups, devices, inputs_ref, w_in_ref, w_rec_ref, bias_ref, h_start_ref, c_start_ref,
    hidden_ref, cell_ref,
    weights, held, gates, recv_sem, send_sem, pass_sem, weight_sem,
):
    steps, batch, local = hidden_ref.shape
    chips = devices // 2
    layer = lax.axis_index("layer")
    me = lax.axis_index("col")
    chip, core = me // 2, lax.rem(me, 2)
    sibling = 2 * chip + 1 - core
    has_left, has_right = chip > 0, chip < chips - 1
    has_prev, has_next = layer > 0, layer < groups - 1

    partners = (
        (has_left, layer, me - 2),
        (has_right, layer, me + 2),
        (None, layer, sibling),
        (has_next, layer + 1, me),
        (has_prev, layer - 1, me),
    )

    def when(condition, action):
        if condition is None:
            action()
        else:
            pl.when(condition)(action)

    def weight_copy(kind, block):
        rows = pl.ds(pl.multiple_of(block * local, local), local)
        source = w_rec_ref if kind == 0 else w_in_ref
        return pltpu.make_async_copy(
            source.at[rows, :], weights.at[kind, rows, :], weight_sem.at[kind, block]
        )

    def input_copy(step, block):
        columns = pl.ds(pl.multiple_of(block * local, local), local)
        return pltpu.make_async_copy(
            inputs_ref.at[step, :, columns], held.at[1, step, block], recv_sem.at[1, step, block]
        )

    start_copy = pltpu.make_async_copy(h_start_ref, held.at[0, 0, me], recv_sem.at[0, 0, me])
    start_copy.start()

    @pl.loop(0, devices)
    def _(block):
        weight_copy(0, block).start()

    @pl.when(layer == 0)
    def _():
        @pl.loop(0, devices)
        def _(block):
            input_copy(0, block).start()

    @pl.loop(0, devices)
    def _(block):
        weight_copy(1, block).start()

    @pl.when(layer == 0)
    def _():
        @pl.loop(1, steps)
        def _(step):
            @pl.loop(0, devices)
            def _(block):
                input_copy(step, block).start()

    barrier = pltpu.get_barrier_semaphore()
    expected = jnp.int32(0)
    for condition, there, col in partners:
        expected = expected + (1 if condition is None else condition.astype(jnp.int32))

        def greet(there=there, col=col):
            pl.semaphore_signal(barrier, inc=1, device_id=(there, col), device_id_type=MESH)

        when(condition, greet)
    pl.semaphore_wait(barrier, expected)

    def hidden_copy(slot, block, way):
        _, there, col = partners[way]
        target = held.at[1, slot - 1, block] if way == NEXT else held.at[0, slot, block]
        arrival = recv_sem.at[1, slot - 1, block] if way == NEXT else recv_sem.at[0, slot, block]
        return pltpu.make_async_remote_copy(
            src_ref=held.at[0, slot, block],
            dst_ref=target,
            send_sem=send_sem.at[slot, block // 2, way],
            recv_sem=arrival,
            device_id=(there, col),
            device_id_type=MESH,
        )

    def source_copy(slot, block):
        return pltpu.make_async_remote_copy(
            src_ref=held.at[1, slot, block],
            dst_ref=held.at[1, slot, block],
            send_sem=pass_sem.at[slot, block // 2],
            recv_sem=recv_sem.at[1, slot, block],
            device_id=(layer, sibling),
            device_id_type=MESH,
        )

    def arrived(kind, slot, block):
        pltpu.make_async_copy(
            held.at[kind, slot, block], held.at[kind, slot, block], recv_sem.at[kind, slot, block]
        ).wait()

    def ways_of(slot, owner):
        return (
            (LEFT, jnp.logical_and(has_left, owner >= chip)),
            (RIGHT, jnp.logical_and(has_right, owner <= chip)),
            (SIBLING, slot < steps),
            (NEXT, jnp.logical_and(has_next, slot >= 1)),
        )

    start_copy.wait()
    cell_ref[...] = c_start_ref[...]

    def multiply(kind, slot, block):
        rows = pl.ds(pl.multiple_of(block * local, local), local)
        gates[...] += jnp.dot(
            held[kind, slot, block], weights[kind, rows, :], preferred_element_type=jnp.float32
        )

    def turn(slot, _):
        compute = slot < steps
        first = slot == 0

        @pl.when(compute)
        def _():
            gates[...] = jnp.broadcast_to(bias_ref[...], gates.shape)

        def event(index, _):
            place = jnp.where(first, lax.rem(index, 4 * chips), index)
            kind = jnp.where(first, index // (4 * chips), lax.rem(index // 2, 2))
            away = jnp.where(first, place // 4, place // 8)
            passed = jnp.where(first, lax.rem(place // 2, 2), lax.rem(place // 4, 2))
            upward = lax.rem(index, 2)
            owner = jnp.where(upward == 0, chip - away, chip + away)
            block = 2 * owner + jnp.where(passed == 0, core, 1 - core)
            valid = jnp.logical_and(owner >= 0, owner < chips)
            valid = jnp.logical_and(valid, jnp.logical_or(away > 0, upward == 0))
            valid = jnp.logical_and(
                valid, jnp.logical_or(compute, jnp.logical_and(kind == 0, passed == 0))
            )

            @pl.when(valid)
            def _():
                mine = jnp.logical_and(kind == 0, jnp.logical_and(away == 0, passed == 0))

                @pl.when(jnp.logical_not(mine))
                def _():
                    arrived(kind, slot, block)

                @pl.when(jnp.logical_and(kind == 0, passed == 0))
                def _():
                    for way, condition in ways_of(slot, owner):
                        pl.when(condition)(lambda way=way: hidden_copy(slot, block, way).start())

                @pl.when(jnp.logical_and(kind == 1, jnp.logical_and(passed == 0, has_prev)))
                def _():
                    source_copy(slot, block).start()

                for which in range(2):
                    @pl.when(jnp.logical_and(first, kind == which))
                    def _():
                        weight_copy(which, block).wait()

                @pl.when(compute)
                def _():
                    multiply(kind, slot, block)

            return 0

        lax.fori_loop(0, 8 * chips, event, 0)

        @pl.when(compute)
        def _():
            part = 16

            def rows_of(index, _):
                rows = pl.ds(pl.multiple_of(index * part, part), part)

                def gate(which):
                    return gates[rows, which * local : (which + 1) * local]

                cell = jax.nn.sigmoid(gate(1)) * cell_ref[rows, :] + jax.nn.sigmoid(
                    gate(0)
                ) * jnp.tanh(gate(2))
                cell_ref[rows, :] = cell
                hidden = (jax.nn.sigmoid(gate(3)) * jnp.tanh(cell)).astype(jnp.bfloat16)
                hidden_ref[slot, rows, :] = hidden
                held[0, slot + 1, me, rows, :] = hidden
                return 0

            lax.fori_loop(0, batch // part, rows_of, 0)

        return 0

    turns = jnp.where(has_next, steps + 1, steps)
    lax.fori_loop(0, turns, turn, 0)

    def drain(slot, _):
        def drain_block(owner, _):
            block = 2 * owner + core
            for way, condition in ways_of(slot, owner):
                pl.when(condition)(lambda way=way: hidden_copy(slot, block, way).wait_send())

            @pl.when(jnp.logical_and(has_prev, slot < steps))
            def _():
                source_copy(slot, block).wait_send()

            return 0

        return lax.fori_loop(0, chips, drain_block, 0)

    lax.fori_loop(0, turns, drain, 0)


def body(inputs, w_input, w_recur, bias, h_start, c_start):
    steps, batch, width = inputs.shape
    local = w_input.shape[3]
    groups = lax.axis_size("layer")
    devices = lax.axis_size("col")
    vmem = pl.BlockSpec(memory_space=pltpu.VMEM)
    anywhere = pl.BlockSpec(memory_space=pl.ANY)
    hidden, cell = pl.pallas_call(
        functools.partial(kernel, groups, devices),
        out_shape=(
            jax.ShapeDtypeStruct((steps, batch, local), jnp.bfloat16),
            jax.ShapeDtypeStruct((batch, local), jnp.float32),
        ),
        in_specs=[anywhere, anywhere, anywhere, vmem, anywhere, vmem],
        out_specs=(vmem, vmem),
        scratch_shapes=[
            pltpu.VMEM((2, width, 4 * local), jnp.bfloat16),
            pltpu.VMEM((2, steps + 1, devices, batch, local), jnp.bfloat16),
            pltpu.VMEM((batch, 4 * local), jnp.float32),
            pltpu.SemaphoreType.DMA((2, steps + 1, devices)),
            pltpu.SemaphoreType.DMA((steps + 1, devices // 2, 4)),
            pltpu.SemaphoreType.DMA((steps, devices // 2)),
            pltpu.SemaphoreType.DMA((2, devices)),
        ],
        compiler_params=pltpu.CompilerParams(
            collective_id=0, has_side_effects=True, vmem_limit_bytes=60 * 1024 * 1024
        ),
    )(
        inputs,
        w_input[0].reshape(width, 4 * local),
        w_recur[0].reshape(width, 4 * local),
        bias[0].reshape(1, 4 * local),
        h_start[0],
        c_start[0],
    )
    return (hidden[None], cell[None])


def solution(mesh):
    in_specs = (
        P(),
        P("layer", None, None, "col"),
        P("layer", None, None, "col"),
        P("layer", None, "col"),
        P("layer", None, "col"),
        P("layer", None, "col"),
    )
    out_specs = (P("layer", None, None, "col"), P("layer", None, "col"))
    return jax.shard_map(body, mesh=mesh, in_specs=in_specs, out_specs=out_specs, check_vma=False)
```

time: 459 us -> 174 us (0.38); the launches traced: 450 us -> 174 us
  waiting for transfers between devices: 196 us -> 0 us
  Pallas kernels: 0 us -> 141 us
  matrix products: 131 us -> 0 us
  local copies, waits for them, and re-layouts: 75.8 us -> 32.1 us
  other arithmetic: 22.3 us -> 0 us
  between operations: 14.5 us -> 0.64 us
  starting transfers between devices: 10.1 us -> 0 us
    all_gather x13 -> x0, waiting for transfers between devices: 159 us -> none  [the longest x6 84 us: body(): arrived = lax.all_gather(received, 'col', axis=2, tiled=True)]
    pallas_call x0 -> x1, Pallas kernels: none -> 141 us  [body(): pl.pallas_call(functools.partial(kernel, groups, devices), out_shape=(jax...]
    dot_general x14 -> x0, matrix products: 131 us -> none  [the longest x7 67.5 us: body(): jnp.dot(source.reshape(span * batch, width), weight_in, preferred_element...]
    ppermute x6 -> x0, waiting for transfers between devices: 36.8 us -> none  [passed_along(): lax.ppermute(value, axis, [(source, source + steps) for source in range(f...]
    slice x7 -> x0, local copies, waits for them, and re-layouts: 23.6 us -> none  [the longest x5 16 us: advance(): gates[:, 0]]
    reshape x7 -> x0, local copies, waits for them, and re-layouts: 17 us -> none  [advance(): gates = gates.reshape(batch, 4, local)]
    select_n x11 -> x0, other arithmetic: 12.1 us -> none  [the longest x7 7.85 us: body(): jnp.where(valid, lax.dynamic_update_slice_in_dim(sequence, shards, start,...]
    convert_element_type x6 -> x0, other arithmetic: 10.2 us -> none  [advance(): (jax.nn.sigmoid(gates[:, 3]) * jnp.tanh(cell_new)).astype(jnp.bfloat16)]
  transfers between devices with their start and end apart: 19 -> 0, of which waited for: 18 -> 0; matrix products, arithmetic and copies ran while one was open for 23% -> 0% of each run, Pallas kernels for 0% -> 0%
where the time goes in v1:
time: 174 us
  Pallas kernels  141 us (81%)
  local copies, waits for them, and re-layouts  32.1 us (18%)
    pallas_call x1, Pallas kernels, body(): pl.pallas_call(functools.partial(kernel, groups, devices), out_shape=(jax...  141 us
    unnamed x7, local copies, waits for them, and re-layouts  32.1 us

profile of v1, /device:TPU:6, one launch (start us, length us, event | category | flops | bytes accessed | tf_op | source)
XLA Modules:
  0.0 173.7 jit_solution(10519568110188155267)
XLA Ops:
  0.6 1.3 copy.10
  1.9 0.0 copy-start
  1.9 18.0 %copy.8 = bf16[512,8,4,512]{3,1,2,0:T(8,128)(2,1)} copy(bf16[512,8,4,512]{3,2,1,0:T(4,128)(2,1)} %bitcast.14) | data formatting | bytes 33554432
  19.9 0.0 copy-done
  19.9 9.3 %copy.9 = bf16[512,8,4,512]{3,1,2,0:T(8,128)(2,1)} copy(bf16[512,8,4,512]{3,2,1,0:T(4,128)(2,1)S(1)} %bitcast.15) | data formatting | bytes 33554432
  29.2 141.0 %shard_map.77 = (bf16[4,128,512]{2,1,0:T(8,128)(2,1)}, f32[128,512]{1,0:T(8,128)}) custom-call(bf16[4,128,4096]{2,1,0:T(8,128)(2,1)} %inputs_ref.1, bf16[4096,2048]{1,0:T(8,128)(2,1)} %bitcast.12, bf16[4096,2048]{1,0:T(8,128)(2,1)} %bitcast.13, f32[1,2048]{1,0:T(1,128)} %bitcast.20, bf16[128,512]{1,0:T(8,128)(2,1)} %bitcast.19, f32[128,512]{1,0:T(8,128)} %bitcast.17), custom_call_target="tpu_custom_call" | custom-call | tf_op jit(solution)/shard_map/pallas_call | solution.py:238
  170.2 1.9 %copy.13 = bf16[1,4,128,512]{3,2,1,0:T(8,128)(2,1)} copy(bf16[1,4,128,512]{3,2,1,0:T(8,128)(2,1)} %bitcast.16) | data formatting | bytes 1048576
  172.1 1.7 copy.14
Async XLA Ops:
  1.9 18.0 %copy-start = (bf16[1,4096,4,512]{3,2,1,0:T(4,128)(2,1)S(1)}, bf16[1,4096,4,512]{3,2,1,0:T(4,128)(2,1)}, u32[]{:S(2)}) copy-start(bf16[1,4096,4,512]{3,2,1,0:T(4,128)(2,1)} %param.8) | copy-start | bytes 50331652

commit v2 on v1

v2 whole, which is shorter than its diff:
```python
import functools

import jax
import jax.numpy as jnp
from jax import lax
from jax.experimental import pallas as pl
from jax.experimental.pallas import tpu as pltpu
from jax.sharding import PartitionSpec as P

MESH = pl.DeviceIdType.MESH
LEFT, RIGHT, SIBLING, NEXT = range(4)


def kernel(
    groups, devices, cuts, inputs_ref, w_in_ref, w_rec_ref, bias_ref, h_start_ref, c_start_ref,
    hidden_ref, cell_ref,
    weights, raw, held, gates, recv_sem, send_sem, pass_sem, raw_sem,
):
    steps, batch, local = hidden_ref.shape
    piece = local // cuts
    chips = devices // 2
    chunks, depth = 2 * devices, raw.shape[0]
    layer = lax.axis_index("layer")
    me = lax.axis_index("col")
    chip, core = me // 2, lax.rem(me, 2)
    sibling = 2 * chip + 1 - core
    has_left, has_right = chip > 0, chip < chips - 1
    has_prev, has_next = layer > 0, layer < groups - 1

    partners = (
        (has_left, layer, me - 2),
        (has_right, layer, me + 2),
        (None, layer, sibling),
        (has_next, layer + 1, me),
        (has_prev, layer - 1, me),
    )

    def when(condition, action):
        if condition is None:
            action()
        else:
            pl.when(condition)(action)

    def raw_copy(source, chunk):
        rows = pl.ds(pl.multiple_of(lax.rem(chunk, devices) * local, local), local)
        slot = lax.rem(chunk, depth)
        return pltpu.make_async_copy(source.at[rows], raw.at[slot], raw_sem.at[slot])

    def raw_start(chunk):
        pl.when(chunk < devices)(lambda: raw_copy(w_rec_ref, chunk).start())
        pl.when(jnp.logical_and(chunk >= devices, chunk < chunks))(
            lambda: raw_copy(w_in_ref, chunk).start()
        )

    def unpack(chunk):
        slot = lax.rem(chunk, depth)
        raw_copy(w_rec_ref, chunk).wait()
        kind, base = chunk // devices, lax.rem(chunk, devices) * local
        part = min(64, local)

        @pl.loop(0, local // part)
        def _(index):
            inner = pl.multiple_of(index * part, part)
            rows = pl.ds(pl.multiple_of(base + inner, part), part)
            weights[kind, rows, :] = raw[slot, pl.ds(inner, part)].reshape(part, 4 * local)

        raw_start(chunk + depth)

    def input_copy(step, block):
        columns = pl.ds(pl.multiple_of(block * piece, piece), piece)
        return pltpu.make_async_copy(
            inputs_ref.at[step, :, columns], held.at[1, step, block], recv_sem.at[1, step, block]
        )

    def start_copy(part):
        columns = slice(part * piece, (part + 1) * piece)
        block = me * cuts + part
        return pltpu.make_async_copy(
            h_start_ref.at[:, columns], held.at[0, 0, block], recv_sem.at[0, 0, block]
        )

    for part in range(cuts):
        start_copy(part).start()

    @pl.loop(0, depth)
    def _(chunk):
        raw_start(chunk)

    @pl.when(layer == 0)
    def _():
        @pl.loop(0, steps)
        def _(step):
            @pl.loop(0, devices * cuts)
            def _(block):
                input_copy(step, block).start()

    barrier = pltpu.get_barrier_semaphore()
    expected = jnp.int32(0)
    for condition, there, col in partners:
        expected = expected + (1 if condition is None else condition.astype(jnp.int32))

        def greet(there=there, col=col):
            pl.semaphore_signal(barrier, inc=1, device_id=(there, col), device_id_type=MESH)

        when(condition, greet)
    pl.semaphore_wait(barrier, expected)

    def hidden_copy(slot, block, way):
        _, there, col = partners[way]
        target = held.at[1, slot - 1, block] if way == NEXT else held.at[0, slot, block]
        arrival = recv_sem.at[1, slot - 1, block] if way == NEXT else recv_sem.at[0, slot, block]
        return pltpu.make_async_remote_copy(
            src_ref=held.at[0, slot, block],
            dst_ref=target,
            send_sem=send_sem.at[slot, place_of(block), way],
            recv_sem=arrival,
            device_id=(there, col),
            device_id_type=MESH,
        )

    def place_of(block):
        return block // (2 * cuts) * cuts + lax.rem(block, cuts)

    def source_copy(slot, block):
        return pltpu.make_async_remote_copy(
            src_ref=held.at[1, slot, block],
            dst_ref=held.at[1, slot, block],
            send_sem=pass_sem.at[slot, place_of(block)],
            recv_sem=recv_sem.at[1, slot, block],
            device_id=(layer, sibling),
            device_id_type=MESH,
        )

    def arrived(kind, slot, block):
        pltpu.make_async_copy(
            held.at[kind, slot, block], held.at[kind, slot, block], recv_sem.at[kind, slot, block]
        ).wait()

    def ways_of(slot, owner):
        wanted = jnp.logical_or(slot < steps, has_next)
        return (
            (LEFT, jnp.logical_and(wanted, jnp.logical_and(has_left, owner >= chip))),
            (RIGHT, jnp.logical_and(wanted, jnp.logical_and(has_right, owner <= chip))),
            (NEXT, jnp.logical_and(has_next, slot >= 1)),
            (SIBLING, slot < steps),
        )

    def send_hidden(slot, owner, block):
        for way, condition in ways_of(slot, owner):
            pl.when(condition)(lambda way=way: hidden_copy(slot, block, way).start())

    cell_ref[...] = c_start_ref[...]

    for part in range(cuts):
        start_copy(part).wait()
        send_hidden(0, chip, me * cuts + part)

    def opening(index, _):
        away, passed, upward = index // 4, lax.rem(index // 2, 2), lax.rem(index, 2)
        owner = jnp.where(upward == 0, chip - away, chip + away)
        col = 2 * owner + jnp.where(passed == 0, core, 1 - core)
        valid = jnp.logical_and(owner >= 0, owner < chips)
        valid = jnp.logical_and(valid, jnp.logical_or(away > 0, upward == 0))
        valid = jnp.logical_and(valid, jnp.logical_or(away > 0, passed == 1))

        @pl.when(valid)
        def _():
            for part in range(cuts):
                block = col * cuts + part
                arrived(0, 0, block)
                pl.when(passed == 0)(lambda block=block: send_hidden(0, owner, block))

        unpack(index)
        return 0

    lax.fori_loop(0, chunks, opening, 0)

    def multiply(kind, slot, block):
        rows = pl.ds(pl.multiple_of(block * piece, piece), piece)
        gates[...] += jnp.dot(
            held[kind, slot, block], weights[kind, rows, :], preferred_element_type=jnp.float32
        )

    def turn(slot, _):
        compute = slot < steps
        first = slot == 0
        half, whole = 4 * cuts * chips, 8 * cuts

        @pl.when(compute)
        def _():
            gates[...] = jnp.broadcast_to(bias_ref[...], gates.shape)

        def event(index, _):
            place = jnp.where(first, lax.rem(index, half), index)
            away = jnp.where(first, place // (4 * cuts), place // whole)
            place = jnp.where(first, lax.rem(place, 4 * cuts), lax.rem(place, whole))
            kind = jnp.where(first, index // half, lax.rem(place // 2, 2))
            passed = jnp.where(first, place // (2 * cuts), place // (4 * cuts))
            part = jnp.where(first, lax.rem(place // 2, cuts), lax.rem(place // 4, cuts))
            upward = lax.rem(index, 2)
            owner = jnp.where(upward == 0, chip - away, chip + away)
            block = (2 * owner + jnp.where(passed == 0, core, 1 - core)) * cuts + part
            valid = jnp.logical_and(owner >= 0, owner < chips)
            valid = jnp.logical_and(valid, jnp.logical_or(away > 0, upward == 0))
            valid = jnp.logical_and(
                valid, jnp.logical_or(compute, jnp.logical_and(kind == 0, passed == 0))
            )

            @pl.when(valid)
            def _():
                mine = jnp.logical_and(away == 0, passed == 0)
                here = jnp.logical_and(kind == 0, jnp.logical_or(mine, first))

                @pl.when(jnp.logical_not(here))
                def _():
                    arrived(kind, slot, block)

                    @pl.when(jnp.logical_and(kind == 0, passed == 0))
                    def _():
                        send_hidden(slot, owner, block)

                    @pl.when(jnp.logical_and(kind == 1, jnp.logical_and(passed == 0, has_prev)))
                    def _():
                        source_copy(slot, block).start()

                @pl.when(compute)
                def _():
                    multiply(kind, slot, block)

            return 0

        lax.fori_loop(0, 8 * cuts * chips, event, 0)

        @pl.when(compute)
        def _():
            height = 32
            for part in range(cuts):
                columns = slice(part * piece, (part + 1) * piece)

                def rows_of(index, _):
                    rows = pl.ds(pl.multiple_of(index * height, height), height)

                    def gate(which):
                        return gates[
                            rows, which * local + part * piece : which * local + (part + 1) * piece
                        ]

                    cell = jax.nn.sigmoid(gate(1)) * cell_ref[rows, columns] + jax.nn.sigmoid(
                        gate(0)
                    ) * jnp.tanh(gate(2))
                    cell_ref[rows, columns] = cell
                    hidden = (jax.nn.sigmoid(gate(3)) * jnp.tanh(cell)).astype(jnp.bfloat16)
                    hidden_ref[slot, rows, columns] = hidden
                    held[0, slot + 1, me * cuts + part, rows, :] = hidden
                    return 0

                lax.fori_loop(0, batch // height, rows_of, 0)
                send_hidden(slot + 1, chip, me * cuts + part)

        return 0

    turns = jnp.where(has_next, steps + 1, steps)
    lax.fori_loop(0, turns, turn, 0)

    def drain(slot, _):
        def drain_block(index, _):
            owner, part = index // cuts, lax.rem(index, cuts)
            block = (2 * owner + core) * cuts + part
            for way, condition in ways_of(slot, owner):
                pl.when(condition)(lambda way=way: hidden_copy(slot, block, way).wait_send())

            @pl.when(jnp.logical_and(has_prev, slot < steps))
            def _():
                source_copy(slot, block).wait_send()

            return 0

        return lax.fori_loop(0, chips * cuts, drain_block, 0)

    lax.fori_loop(0, turns, drain, 0)


def body(inputs, w_input, w_recur, bias, h_start, c_start):
    steps, batch, width = inputs.shape
    local = w_input.shape[3]
    groups = lax.axis_size("layer")
    devices = lax.axis_size("col")
    cuts = 2 if local % 512 == 0 else 1
    vmem = pl.BlockSpec(memory_space=pltpu.VMEM)
    anywhere = pl.BlockSpec(memory_space=pl.ANY)
    hidden, cell = pl.pallas_call(
        functools.partial(kernel, groups, devices, cuts),
        out_shape=(
            jax.ShapeDtypeStruct((steps, batch, local), jnp.bfloat16),
            jax.ShapeDtypeStruct((batch, local), jnp.float32),
        ),
        in_specs=[anywhere, anywhere, anywhere, vmem, anywhere, vmem],
        out_specs=(vmem, vmem),
        scratch_shapes=[
            pltpu.VMEM((2, width, 4 * local), jnp.bfloat16),
            pltpu.VMEM((4, local, 4, local), jnp.bfloat16),
            pltpu.VMEM((2, steps + 1, devices * cuts, batch, local // cuts), jnp.bfloat16),
            pltpu.VMEM((batch, 4 * local), jnp.float32),
            pltpu.SemaphoreType.DMA((2, steps + 1, devices * cuts)),
            pltpu.SemaphoreType.DMA((steps + 1, devices // 2 * cuts, 4)),
            pltpu.SemaphoreType.DMA((steps, devices // 2 * cuts)),
            pltpu.SemaphoreType.DMA((4,)),
        ],
        compiler_params=pltpu.CompilerParams(
            collective_id=0, has_side_effects=True, vmem_limit_bytes=60 * 1024 * 1024
        ),
    )(
        inputs,
        w_input[0],
        w_recur[0],
        bias[0].reshape(1, 4 * local),
        h_start[0],
        c_start[0],
    )
    return (hidden[None], cell[None])


def solution(mesh):
    in_specs = (
        P(),
        P("layer", None, None, "col"),
        P("layer", None, None, "col"),
        P("layer", None, "col"),
        P("layer", None, "col"),
        P("layer", None, "col"),
    )
    out_specs = (P("layer", None, None, "col"), P("layer", None, "col"))
    return jax.shard_map(body, mesh=mesh, in_specs=in_specs, out_specs=out_specs, check_vma=False)
```

time: 174 us -> 156 us (0.90)
  local copies, waits for them, and re-layouts: 32.1 us -> 4.84 us
  Pallas kernels: 141 us -> 150 us
    unnamed x7 -> x3, local copies, waits for them, and re-layouts: 32.1 us -> 4.84 us
    pallas_call x1, Pallas kernels: 141 us -> 150 us  [body(): pl.pallas_call(functools.partial(kernel, groups, devices, cuts), out_shap...]
where the time goes in v2:
time: 156 us
  Pallas kernels  150 us (96%)
  local copies, waits for them, and re-layouts  4.84 us (3%)
    pallas_call x1, Pallas kernels, body(): pl.pallas_call(functools.partial(kernel, groups, devices, cuts), out_shap...  150 us
    unnamed x3, local copies, waits for them, and re-layouts  4.84 us

profile of v2, /device:TPU:6, one launch (start us, length us, event | category | flops | bytes accessed | tf_op | source)
XLA Modules:
  0.0 155.8 jit_solution(18197925799191032249)
XLA Ops:
  0.6 1.3 copy.8
  1.9 150.3 %shard_map.77 = (bf16[4,128,512]{2,1,0:T(8,128)(2,1)}, f32[128,512]{1,0:T(8,128)}) custom-call(bf16[4,128,4096]{2,1,0:T(8,128)(2,1)} %inputs_ref.1, bf16[4096,4,512]{2,1,0:T(4,128)(2,1)} %bitcast.8, bf16[4096,4,512]{2,1,0:T(4,128)(2,1)} %bitcast.9, f32[1,2048]{1,0:T(1,128)} %bitcast.14, bf16[128,512]{1,0:T(8,128)(2,1)} %bitcast.13, f32[128,512]{1,0:T(8,128)} %bitcast.11), custom_call_target="tpu_custom_call" | custom-call | tf_op jit(solution)/shard_map/pallas_call | solution.py:291
  152.3 1.9 %copy.11 = bf16[1,4,128,512]{3,2,1,0:T(8,128)(2,1)} copy(bf16[1,4,128,512]{3,2,1,0:T(8,128)(2,1)} %bitcast.10) | data formatting | bytes 1048576
  154.1 1.7 %copy.12 = f32[1,128,512]{2,1,0:T(8,128)} copy(f32[1,128,512]{2,1,0:T(8,128)} %bitcast.12) | data formatting | bytes 524288

commit v3 on v2

--- a/solution.py
+++ b/solution.py
@@ -47,15 +47,15 @@
         return pltpu.make_async_copy(source.at[rows], raw.at[slot], raw_sem.at[slot])
 
     def raw_start(chunk):
-        pl.when(chunk < devices)(lambda: raw_copy(w_rec_ref, chunk).start())
+        pl.when(chunk < devices)(lambda: raw_copy(w_in_ref, chunk).start())
         pl.when(jnp.logical_and(chunk >= devices, chunk < chunks))(
-            lambda: raw_copy(w_in_ref, chunk).start()
+            lambda: raw_copy(w_rec_ref, chunk).start()
         )
 
     def unpack(chunk):
         slot = lax.rem(chunk, depth)
         raw_copy(w_rec_ref, chunk).wait()
-        kind, base = chunk // devices, lax.rem(chunk, devices) * local
+        kind, base = 1 - chunk // devices, lax.rem(chunk, devices) * local
         part = min(64, local)
 
         @pl.loop(0, local // part)
@@ -155,6 +155,12 @@
         start_copy(part).wait()
         send_hidden(0, chip, me * cuts + part)
 
+    def multiply(kind, slot, block):
+        rows = pl.ds(pl.multiple_of(block * piece, piece), piece)
+        gates[...] += jnp.dot(
+            held[kind, slot, block], weights[kind, rows, :], preferred_element_type=jnp.float32
+        )
+
     def opening(index, _):
         away, passed, upward = index // 4, lax.rem(index // 2, 2), lax.rem(index, 2)
         owner = jnp.where(upward == 0, chip - away, chip + away)
@@ -171,22 +177,26 @@
                 pl.when(passed == 0)(lambda block=block: send_hidden(0, owner, block))
 
         unpack(index)
+
+        @pl.when(jnp.logical_and(layer == 0, index >= devices))
+        def _():
+            @pl.loop(0, cuts)
+            def _(part):
+                ready = (index - devices) * cuts + part
+                arrived(1, 0, ready)
+                multiply(1, 0, ready)
+
         return 0
 
+    gates[...] = jnp.broadcast_to(bias_ref[...], gates.shape)
     lax.fori_loop(0, chunks, opening, 0)
-
-    def multiply(kind, slot, block):
-        rows = pl.ds(pl.multiple_of(block * piece, piece), piece)
-        gates[...] += jnp.dot(
-            held[kind, slot, block], weights[kind, rows, :], preferred_element_type=jnp.float32
-        )
 
     def turn(slot, _):
         compute = slot < steps
         first = slot == 0
         half, whole = 4 * cuts * chips, 8 * cuts
 
-        @pl.when(compute)
+        @pl.when(jnp.logical_and(compute, jnp.logical_not(first)))
         def _():
             gates[...] = jnp.broadcast_to(bias_ref[...], gates.shape)
 
@@ -198,6 +208,8 @@
             passed = jnp.where(first, place // (2 * cuts), place // (4 * cuts))
             part = jnp.where(first, lax.rem(place // 2, cuts), lax.rem(place // 4, cuts))
             upward = lax.rem(index, 2)
+            late = jnp.logical_and(passed == 1, jnp.logical_not(first))
+            away = jnp.where(late, away - 1, away)
             owner = jnp.where(upward == 0, chip - away, chip + away)
             block = (2 * owner + jnp.where(passed == 0, core, 1 - core)) * cuts + part
             valid = jnp.logical_and(owner >= 0, owner < chips)
@@ -206,6 +218,10 @@
                 valid, jnp.logical_or(compute, jnp.logical_and(kind == 0, passed == 0))
             )
 
+            valid = jnp.logical_and(valid, jnp.logical_and(away >= 0, jnp.logical_or(index < 2 * half, jnp.logical_not(first))))
+            ahead = jnp.logical_and(jnp.logical_and(layer == 0, first), kind == 1)
+            valid = jnp.logical_and(valid, jnp.logical_not(ahead))
+
             @pl.when(valid)
             def _():
                 mine = jnp.logical_and(away == 0, passed == 0)
@@ -229,7 +245,7 @@
 
             return 0
 
-        lax.fori_loop(0, 8 * cuts * chips, event, 0)
+        lax.fori_loop(0, 8 * cuts * (chips + 1), event, 0)
 
         @pl.when(compute)
         def _():
@@ -285,7 +301,7 @@
     local = w_input.shape[3]
     groups = lax.axis_size("layer")
     devices = lax.axis_size("col")
-    cuts = 2 if local % 512 == 0 else 1
+    cuts = 1
     vmem = pl.BlockSpec(memory_space=pltpu.VMEM)
     anywhere = pl.BlockSpec(memory_space=pl.ANY)
     hidden, cell = pl.pallas_call(

time: 156 us -> 142 us (0.910)
  Pallas kernels: 150 us -> 137 us
    pallas_call x1, Pallas kernels: 150 us -> 137 us  [body(): pl.pallas_call(functools.partial(kernel, groups, devices, cuts), out_shap...]
where the time goes in v3:
time: 142 us
  Pallas kernels  137 us (96%)
  local copies, waits for them, and re-layouts  4.84 us (3%)
    pallas_call x1, Pallas kernels, body(): pl.pallas_call(functools.partial(kernel, groups, devices, cuts), out_shap...  137 us
    unnamed x3, local copies, waits for them, and re-layouts  4.84 us

profile of v3, /device:TPU:6, one launch (start us, length us, event | category | flops | bytes accessed | tf_op | source)
XLA Modules:
  0.0 142.1 jit_solution(7924539653274744834)
XLA Ops:
  0.6 1.3 copy.8
  1.9 136.6 %shard_map.77 = (bf16[4,128,512]{2,1,0:T(8,128)(2,1)}, f32[128,512]{1,0:T(8,128)}) custom-call(bf16[4,128,4096]{2,1,0:T(8,128)(2,1)} %inputs_ref.1, bf16[4096,4,512]{2,1,0:T(4,128)(2,1)} %bitcast.8, bf16[4096,4,512]{2,1,0:T(4,128)(2,1)} %bitcast.9, f32[1,2048]{1,0:T(1,128)} %bitcast.14, bf16[128,512]{1,0:T(8,128)(2,1)} %bitcast.13, f32[128,512]{1,0:T(8,128)} %bitcast.11), custom_call_target="tpu_custom_call" | custom-call | tf_op jit(solution)/shard_map/pallas_call | solution.py:307
  138.5 1.9 %copy.11 = bf16[1,4,128,512]{3,2,1,0:T(8,128)(2,1)} copy(bf16[1,4,128,512]{3,2,1,0:T(8,128)(2,1)} %bitcast.10) | data formatting | bytes 1048576
  140.4 1.7 %copy.12 = f32[1,128,512]{2,1,0:T(8,128)} copy(f32[1,128,512]{2,1,0:T(8,128)} %bitcast.12) | data formatting | bytes 524288
